TPU v7x, 32 devices: a whole 2x2x4 slice. The times are simulated.
32 devices in a mesh: exp: 8 (over y, x, core), tp: 4 (over z).
Axes of the slice: x: 2, y: 2, z: 4, core: 2. Of those that a mesh axis runs over, the one named last changes fastest.
Arguments:
- attn_part: bfloat16 [4, 256, 7168], P('tp', 'exp'), may hold values from -2.5 to 2.5
- resid: bfloat16 [256, 7168], P('exp', 'tp'), may hold values from -50 to 50
- refusal: float32 [7168], replicated, may hold values from -4 to 4
- norm_gain: float32 [7168], P('tp'), may hold values from 0.5 to 1.5
- route_ids: int32 [256, 8], P('exp'), may hold values from 0 to 31, all different within a row; in each aligned block of 32 rows (0 to 31, 32 to 63, ...) at most 16 rows name the same one
- gate_q: int32 [256, 8], P('exp'), may hold values from 16 to 255
- w_gate: bfloat16 [32, 7168, 2048], P('exp', None, 'tp'), may hold values from -0.0625 to 0.0625
- w_up: bfloat16 [32, 7168, 2048], P('exp', None, 'tp'), may hold values from -0.0625 to 0.0625
- w_down: bfloat16 [32, 2048, 7168], P('exp', 'tp'), may hold values from -0.125 to 0.125
Outputs:
- layer_out: bfloat16 [256, 7168], P('exp', 'tp')
Inputs may be any that keep to these rules, and one draw needn't show every extreme that they name: `route_ids`: each row names 8 different experts; in each aligned block of 32 rows (the tokens of one index of exp) no expert is named by more than 16 rows, a bound that some block reaches.
All inputs are finite; a program needn't handle non-finite values.
Results may differ from a plain program's by a relative error of at most 0.015.
Values may be sent and summed in bfloat16 or wider, within the bound.
No kernel may reach another device: no remote copies, remote signals or barrier semaphores. Data moves between devices by JAX's collectives and lax.ppermute only.
A program may use at most 256 MiB of HBM per device.

v0:
```python
import jax
import jax.numpy as jnp
from jax import lax
from jax.sharding import PartitionSpec as P

CAP = 16
EPSILON = 1e-06
GATE_UNIT = 128.0


def route_tables(route_ids, gate_q, experts, slot_count):
    row_count = route_ids.shape[0]
    matches = route_ids[:, :, None] == jnp.arange(experts, dtype=jnp.int32)[None, None, :]
    named_count = jnp.sum(matches.astype(jnp.int32), axis=1, dtype=jnp.int32)
    weight = jnp.sum(jnp.where(matches, gate_q[:, :, None], 0), axis=1, dtype=jnp.int32)
    before = jnp.cumsum(named_count, axis=0, dtype=jnp.int32) - named_count
    placed = (named_count[:, :, None] == 1) & (
        before[:, :, None] == jnp.arange(slot_count, dtype=jnp.int32)[None, None, :]
    )
    select = placed.reshape(row_count, experts * slot_count)
    scaled = jnp.where(placed, weight[:, :, None].astype(jnp.float32) / GATE_UNIT, 0.0)
    scaled = scaled.reshape(row_count, experts * slot_count)
    return (select.astype(jnp.bfloat16).T, scaled.astype(jnp.bfloat16))


def apply_experts(inputs, gate_weight, up_weight, down_weight):
    gate_act = jnp.einsum("sicd,idh->sich", inputs, gate_weight, preferred_element_type=jnp.float32)
    up_act = jnp.einsum("sicd,idh->sich", inputs, up_weight, preferred_element_type=jnp.float32)
    activation = (jax.nn.silu(gate_act) * up_act).astype(jnp.bfloat16)
    term = jnp.einsum("sich,ihd->sicd", activation, down_weight, preferred_element_type=jnp.float32)
    return term.astype(jnp.bfloat16)


def local(attn_part, resid, refusal, norm_gain, route_ids, gate_q, w_gate, w_up, w_down):
    highest = lax.Precision.HIGHEST
    tp_count = lax.axis_size("tp")
    exp_count = lax.axis_size("exp")
    full_width = refusal.shape[0]
    col_count = full_width // tp_count
    local_experts = w_gate.shape[0]
    experts = local_experts * exp_count
    attn_summed = lax.psum_scatter(
        attn_part[0].astype(jnp.float32).astype(jnp.bfloat16), "tp", scatter_dimension=1, tiled=True
    ).astype(jnp.float32)
    summed_heads = resid.astype(jnp.float32) + attn_summed
    unit = refusal * lax.rsqrt(jnp.sum(refusal * refusal) + EPSILON)
    unit_cols = lax.dynamic_slice_in_dim(unit, lax.axis_index("tp") * col_count, col_count, 0)
    along_part = jnp.dot(summed_heads, unit_cols, precision=highest)
    along, energy = lax.psum((along_part, jnp.sum(summed_heads * summed_heads, axis=1)), "tp")
    projected = summed_heads - along[:, None] * unit_cols[None, :]
    squares = energy - along * along * (2.0 - jnp.sum(unit * unit))
    inverse = lax.rsqrt(squares / full_width + EPSILON)
    normed = (projected * inverse[:, None] * norm_gain[None, :]).astype(jnp.bfloat16)
    select, scaled = route_tables(route_ids, gate_q, experts, CAP)
    full_rows = lax.all_gather(normed, "tp", axis=1, tiled=True)
    outgoing = jnp.dot(select, full_rows, preferred_element_type=jnp.float32).astype(jnp.bfloat16)
    outgoing = outgoing.reshape(exp_count, local_experts, CAP, full_width)
    expert_terms = apply_experts(
        lax.all_to_all(outgoing, "exp", split_axis=0, concat_axis=0, tiled=True),
        w_gate,
        w_up,
        w_down,
    )
    returned = lax.all_to_all(expert_terms, "exp", split_axis=0, concat_axis=0, tiled=True)
    partial_sum = jnp.dot(
        scaled, returned.reshape(experts * CAP, full_width), preferred_element_type=jnp.float32
    )
    mixed_cols = lax.psum_scatter(
        partial_sum.astype(jnp.bfloat16), "tp", scatter_dimension=1, tiled=True
    ).astype(jnp.float32)
    return (projected + mixed_cols).astype(jnp.bfloat16)


def solution(mesh):
    return jax.shard_map(
        local,
        mesh=mesh,
        in_specs=(
            P("tp", "exp", None),
            P("exp", "tp"),
            P(),
            P("tp"),
            P("exp", None),
            P("exp", None),
            P("exp", None, "tp"),
            P("exp", None, "tp"),
            P("exp", "tp", None),
        ),
        out_specs=P("exp", "tp"),
        check_vma=False,
    )
```

profile of v0, /device:TPU:0, one launch (start us, length us, event | category | flops | bytes accessed | tf_op | source)
XLA Modules:
  0.0 321.4 jit_solution(12197363555979041016)
XLA Ops:
  6.5 0.0 reduce-scatter.3.cloned.1.call-start
  6.5 0.7 reduce-scatter.3.cloned.1.call-update
  7.3 1.4 multiply_reduce_fusion.2
  9.3 1.4 multiply_reduce_fusion.1
  10.7 0.1 dynamic_slice.3
  10.8 0.8 copy.26
  11.5 0.8 copy.29
  12.3 0.2 convert_reduce_fusion
  12.4 0.1 reduce_window_sum.11
  12.5 0.1 copy.28
  12.6 0.1 copy.27
  12.7 0.1 eq.66
  13.4 0.1 fusion.35
  13.6 19.8 %reduce-scatter.3.cloned.1.call-done = bf16[32,1792]{1,0:T(8,128)(2,1)} async-done(((bf16[32,7168]{1,0:T(8,128)(2,1)}), bf16[32,1792]{1,0:T(8,128)(2,1)}) %reduce-scatter.3.cloned.1.call-update) | async-done | bytes 114704 | tf_op jit(solution)/shard_map/reduce_scatter | solution.py:42
  33.4 1.1 multiply_reduce_fusion
  34.5 1.2 convolution_bitcast_fusion
  35.7 8.7 %all-reduce = (f32[32]{0:T(128)S(1)}, f32[32]{0:T(128)S(1)}) all-reduce(f32[32]{0:T(128)S(1)} %multiply_reduce_fusion, f32[32]{0:T(128)S(1)} %convolution_bitcast_fusion), channel_id=1, replica_groups=mesh['exp'=8,'tp'=4] {'tp'}, use_global_device_ids=true, to_apply=%region_7.8 | all-reduce | flops 64 | bytes 512 | tf_op jit(solution)/shard_map/psum | solution.py:49
  44.4 1.1 multiply_convert_fusion
  45.5 14.5 %all_gather.3 = bf16[32,7168]{1,0:T(8,128)(2,1)S(1)} all-gather(bf16[32,1792]{1,0:T(8,128)(2,1)S(1)} %multiply_convert_fusion), channel_id=1, replica_groups=mesh['exp'=8,'tp'=4] {'tp'}, dimensions={1}, use_global_device_ids=true | all-gather | bytes 573440 | tf_op jit(solution)/shard_map/all_gather | solution.py:55
  59.9 2.0 convolution_convert_fusion
  62.0 86.6 %all_to_all.10 = bf16[8,4,16,7168]{3,2,1,0:T(8,128)(2,1)} all-to-all(bf16[8,4,16,7168]{3,2,1,0:T(8,128)(2,1)S(1)} %bitcast.55), channel_id=1, replica_groups=mesh['exp'=8,'tp'=4] {'exp'}, dimensions={0} | all-to-all | bytes 14680064 | tf_op jit(solution)/shard_map/all_to_all | solution.py:59
  148.6 13.5 %fusion.14 = f32[8,4,16,512]{3,2,0,1:T(8,128)S(1)} fusion(bf16[4,7168,512]{2,1,0:T(8,128)(2,1)} %param.15, bf16[8,4,16,7168]{3,2,1,0:T(8,128)(2,1)} %all_to_all.10), kind=kOutput, calls=%fused_computation.12 | convolution fusion | flops 3758096384 | bytes 37748736 | tf_op jit(solution)/shard_map/sicd,idh->sich/dot_general | solution.py:27
  162.1 15.5 %fusion.29 = bf16[8,4,16,512]{3,2,0,1:T(8,128)(2,1)S(1)} fusion(bf16[4,7168,512]{2,1,0:T(8,128)(2,1)} %param.16, bf16[8,4,16,7168]{3,2,1,0:T(8,128)(2,1)} %all_to_all.10, f32[8,4,16,512]{3,2,0,1:T(8,128)S(1)} %fusion.14), kind=kOutput, calls=%fused_computation.15 | convolution fusion | flops 3759669248 | bytes 38273024 | tf_op jit(solution)/shard_map/sicd,idh->sich/dot_general | solution.py:28
  177.6 16.3 %fusion.9 = bf16[8,4,16,7168]{3,2,0,1:T(8,128)(2,1)} fusion(bf16[8,4,16,512]{3,2,0,1:T(8,128)(2,1)S(1)} %fusion.29, bf16[4,512,7168]{2,1,0:T(8,128)(2,1)} %param.17), kind=kOutput, calls=%fused_computation.8 | convolution fusion | flops 3761766400 | bytes 37224448 | tf_op jit(solution)/shard_map/sich,ihd->sicd/dot_general | solution.py:30
  194.0 6.9 %copy.33 = bf16[8,4,16,7168]{3,2,1,0:T(8,128)(2,1)} copy(bf16[8,4,16,7168]{3,2,0,1:T(8,128)(2,1)} %fusion.9) | data formatting | bytes 14680064 | tf_op jit(solution)/shard_map/convert_element_type | solution.py:31
  200.8 4.8 %all-to-all-start.1 = ((bf16[8,4,16,7168]{3,2,1,0:T(8,128)(2,1)}), bf16[8,4,16,7168]{3,2,1,0:T(8,128)(2,1)}, u32[]{:S(2)}, u32[]{:S(2)}) async-start(bf16[8,4,16,7168]{3,2,1,0:T(8,128)(2,1)} %copy.33), calls=%async_computation.2 | async-start | bytes 14680064 | tf_op jit(solution)/shard_map/all_to_all | solution.py:64
  205.7 0.0 copy-start
  205.7 0.0 copy-start.1
  205.7 0.0 reduce-scatter.5.cloned.1.call-start
  205.8 0.1 copy.30
  205.8 0.1 select_convert_fusion
  205.9 82.6 %all-to-all-done.1 = bf16[8,4,16,7168]{3,2,1,0:T(8,128)(2,1)} async-done(((bf16[8,4,16,7168]{3,2,1,0:T(8,128)(2,1)}), bf16[8,4,16,7168]{3,2,1,0:T(8,128)(2,1)}, u32[]{:S(2)}, u32[]{:S(2)}) %all-to-all-start.1) | async-done | bytes 7340064 | tf_op jit(solution)/shard_map/all_to_all | solution.py:64
  288.5 5.3 %convolution_convert_fusion.1 = bf16[32,7168]{1,0:T(8,128)(2,1)} fusion(bf16[32,512]{0,1:T(8,128)(2,1)S(1)} %bitcast.56, bf16[512,7168]{1,0:T(8,128)(2,1)} %bitcast.15), kind=kOutput, calls=%fused_computation.9 | convolution fusion | flops 235110400 | bytes 7831552 | tf_op jit(solution)/shard_map/dot_general | solution.py:65
  293.8 0.0 reduce-scatter.5.cloned.1.call-update
  293.8 19.1 %reduce-scatter.5.cloned.1.call-done = bf16[32,1792]{1,0:T(8,128)(2,1)} async-done(((bf16[32,7168]{1,0:T(8,128)(2,1)}), bf16[32,1792]{1,0:T(8,128)(2,1)}) %reduce-scatter.5.cloned.1.call-update) | async-done | bytes 114704 | tf_op jit(solution)/shard_map/reduce_scatter | solution.py:68
  312.9 0.0 copy-done
  312.9 0.0 copy-done.1
  312.9 1.6 add_convert_fusion
  (6 shorter events, 0.0 us)
Async XLA Ops:
  6.5 26.8 %reduce-scatter.3.cloned.1.call-start = ((), (), s32[]{:S(2)}) async-start(), calls=%async_computation.4 | async-start | bytes 573440 | tf_op jit(solution)/shard_map/reduce_scatter | solution.py:42
  200.8 87.7 %all-to-all-start.1 = ((bf16[8,4,16,7168]{3,2,1,0:T(8,128)(2,1)}), bf16[8,4,16,7168]{3,2,1,0:T(8,128)(2,1)}, u32[]{:S(2)}, u32[]{:S(2)}) async-start(bf16[8,4,16,7168]{3,2,1,0:T(8,128)(2,1)} %copy.33), calls=%async_computation.2 | async-start | bytes 14680064 | tf_op jit(solution)/shard_map/all_to_all | solution.py:64
  205.7 107.3 %copy-start = (bf16[32,1792]{1,0:T(8,128)(2,1)S(1)}, bf16[32,1792]{1,0:T(8,128)(2,1)}, u32[]{:S(2)}) copy-start(bf16[32,1792]{1,0:T(8,128)(2,1)} %param.10) | copy-start | bytes 344068
  205.7 107.2 %copy-start.1 = (bf16[32,1792]{1,0:T(8,128)(2,1)S(1)}, bf16[32,1792]{1,0:T(8,128)(2,1)}, u32[]{:S(2)}) copy-start(bf16[32,1792]{1,0:T(8,128)(2,1)} %reduce-scatter.3.cloned.1.call-done) | copy-start | bytes 344068
  205.7 107.2 %reduce-scatter.5.cloned.1.call-start = ((), (), s32[]{:S(2)}) async-start(), calls=%async_computation.5 | async-start | bytes 573440 | tf_op jit(solution)/shard_map/reduce_scatter | solution.py:68
Sparse Core Ops, SparseCore 0:
  9.6 23.6 reduce-scatter.2
  293.9 18.9 reduce-scatter.4
where the time goes:
time: 322 us; the launch traced here: 321 us
  waiting for transfers between devices  122 us (38%)
  blocking collectives  110 us (34%)
  matrix products  53.8 us (17%)
  between operations  14.9 us (5%)
  local copies, waits for them, and re-layouts  8.82 us (3%)
  other arithmetic  6.99 us (2%)
  starting transfers between devices  4.89 us (2%)
    all_to_all x1, blocking collectives, local(): lax.all_to_all(outgoing, 'exp', split_axis=0, concat_axis=0, tiled=True)  86.6 us
    all_to_all x1, waiting for transfers between devices, local(): lax.all_to_all(expert_terms, 'exp', split_axis=0, concat_axis=0, tiled=True)  82.6 us
    reduce_scatter x1, waiting for transfers between devices, local(): lax.psum_scatter(attn_part[0].astype(jnp.float32).astype(jnp.bfloat16), '...  19.8 us
    reduce_scatter x1, waiting for transfers between devices, local(): lax.psum_scatter(partial_sum.astype(jnp.bfloat16), 'tp', scatter_dimensio...  19.1 us
    dot_general x1, matrix products, apply_experts(): jnp.einsum('sich,ihd->sicd', activation, down_weight, preferred_element_t...  16.3 us
    dot_general x1, matrix products, apply_experts(): jnp.einsum('sicd,idh->sich', inputs, up_weight, preferred_element_type=jn...  15.5 us
    all_gather x1, blocking collectives, local(): full_rows = lax.all_gather(normed, 'tp', axis=1, tiled=True)  14.5 us
    dot_general x1, matrix products, apply_experts(): jnp.einsum('sicd,idh->sich', inputs, gate_weight, preferred_element_type=...  13.5 us
  transfers between devices with their start and end apart: 3, of which 3 were waited for; matrix products, arithmetic and copies ran while one was open for 2% of the time, Pallas kernels for 0%

commit v1 on v0

--- a/solution.py
+++ b/solution.py
@@ -2,6 +2,7 @@
 import jax.numpy as jnp
 from jax import lax
 from jax.sharding import PartitionSpec as P
+from jax.lax import axis_index, axis_size, ppermute
 
 CAP = 16
 EPSILON = 1e-06
@@ -52,7 +53,15 @@
     inverse = lax.rsqrt(squares / full_width + EPSILON)
     normed = (projected * inverse[:, None] * norm_gain[None, :]).astype(jnp.bfloat16)
     select, scaled = route_tables(route_ids, gate_q, experts, CAP)
-    full_rows = lax.all_gather(normed, "tp", axis=1, tiled=True)
+    main = axis_size("tp")
+    extra = axis_index("tp")
+    front, big, ready = (main, extra, normed.shape[1])
+    g_now, b_now = (normed, 1)
+    while b_now < front:
+        mat_out = ppermute(g_now, "tp", [(d, (d - b_now) % front) for d in range(front)])
+        g_now = jnp.concatenate([g_now, mat_out], axis=1)
+        b_now = 2 * b_now
+    full_rows = jnp.roll(g_now, big * ready, axis=1)
     outgoing = jnp.dot(select, full_rows, preferred_element_type=jnp.float32).astype(jnp.bfloat16)
     outgoing = outgoing.reshape(exp_count, local_experts, CAP, full_width)
     expert_terms = apply_experts(

time: 322 us -> 325 us (level)
  blocking collectives: 110 us -> 95.1 us
  waiting for transfers between devices: 122 us -> 133 us
  starting transfers between devices: 4.89 us -> 10.7 us
    all_gather x1 -> x0, blocking collectives: 14.5 us -> none  [local(): full_rows = lax.all_gather(normed, 'tp', axis=1, tiled=True)]
    ppermute x0 -> x2, waiting for transfers between devices: none -> 6.75 us  [local(): ppermute(g_now, 'tp', [(d, (d - b_now) % front) for d in range(front)])]
    ppermute x0 -> x2, starting transfers between devices: none -> 5.85 us  [local(): ppermute(g_now, 'tp', [(d, (d - b_now) % front) for d in range(front)])]
    reduce_scatter x1, waiting for transfers between devices: 19.1 us -> 22.8 us  [local(): lax.psum_scatter(partial_sum.astype(jnp.bfloat16), 'tp', scatter_dimensio...]
  transfers between devices with their start and end apart: 3 -> 5, of which waited for: 3 -> 5; matrix products, arithmetic and copies ran while one was open for 2% -> 2% of each run, Pallas kernels for 0% -> 0%
where the time goes in v1:
time: 325 us; the launch traced here: 324 us
  waiting for transfers between devices  133 us (41%)
  blocking collectives  95.1 us (29%)
  matrix products  53.9 us (17%)
  between operations  14.9 us (5%)
  starting transfers between devices  10.7 us (3%)
  local copies, waits for them, and re-layouts  8.88 us (3%)
  other arithmetic  7.03 us (2%)
    all_to_all x1, blocking collectives, local(): lax.all_to_all(outgoing, 'exp', split_axis=0, concat_axis=0, tiled=True)  86.4 us
    all_to_all x1, waiting for transfers between devices, local(): lax.all_to_all(expert_terms, 'exp', split_axis=0, concat_axis=0, tiled=True)  82.6 us
    reduce_scatter x1, waiting for transfers between devices, local(): lax.psum_scatter(partial_sum.astype(jnp.bfloat16), 'tp', scatter_dimensio...  22.8 us
    reduce_scatter x1, waiting for transfers between devices, local(): lax.psum_scatter(attn_part[0].astype(jnp.float32).astype(jnp.bfloat16), '...  20.4 us
    dot_general x1, matrix products, apply_experts(): jnp.einsum('sich,ihd->sicd', activation, down_weight, preferred_element_t...  16.3 us
    dot_general x1, matrix products, apply_experts(): jnp.einsum('sicd,idh->sich', inputs, up_weight, preferred_element_type=jn...  15.5 us
    dot_general x1, matrix products, apply_experts(): jnp.einsum('sicd,idh->sich', inputs, gate_weight, preferred_element_type=...  13.5 us
    psum x1, blocking collectives, local(): lax.psum((along_part, jnp.sum(summed_heads * summed_heads, axis=1)), 'tp')  8.7 us
  transfers between devices with their start and end apart: 5, of which 5 were waited for; matrix products, arithmetic and copies ran while one was open for 2% of the time, Pallas kernels for 0%

profile of v1, /device:TPU:0, one launch (start us, length us, event | category | flops | bytes accessed | tf_op | source)
XLA Modules:
  0.0 323.8 jit_solution(11772610131547825813)
XLA Ops:
  6.5 0.0 reduce-scatter.3.cloned.1.call-start
  6.5 0.7 reduce-scatter.3.cloned.1.call-update
  7.3 1.4 multiply_reduce_fusion.2
  9.3 1.4 multiply_reduce_fusion.1
  10.7 0.1 dynamic_slice.7
  10.8 0.8 copy.26
  11.5 0.8 copy.29
  12.9 20.4 %reduce-scatter.3.cloned.1.call-done = bf16[32,1792]{1,0:T(8,128)(2,1)} async-done(((bf16[32,7168]{1,0:T(8,128)(2,1)}), bf16[32,1792]{1,0:T(8,128)(2,1)}) %reduce-scatter.3.cloned.1.call-update) | async-done | bytes 114704 | tf_op jit(solution)/shard_map/reduce_scatter | solution.py:43
  33.4 1.1 multiply_reduce_fusion
  34.5 1.2 convolution_bitcast_fusion
  35.7 8.7 %all-reduce = (f32[32]{0:T(128)S(1)}, f32[32]{0:T(128)S(1)}) all-reduce(f32[32]{0:T(128)S(1)} %multiply_reduce_fusion, f32[32]{0:T(128)S(1)} %convolution_bitcast_fusion), channel_id=1, replica_groups=mesh['exp'=8,'tp'=4] {'tp'}, use_global_device_ids=true, to_apply=%region_7.8 | all-reduce | flops 64 | bytes 512 | tf_op jit(solution)/shard_map/psum | solution.py:50
  44.4 1.1 constant_dynamic-update-slice_fusion.5
  45.5 1.8 collective-permute-start
  47.3 0.2 convert_reduce_fusion
  47.4 3.2 %collective-permute-done = bf16[32,1792]{1,0:T(8,128)(2,1)S(1)} collective-permute-done((bf16[32,1792]{1,0:T(8,128)(2,1)S(1)}, bf16[32,1792]{1,0:T(8,128)(2,1)S(1)}, u32[]{:S(2)}, u32[]{:S(2)}) %collective-permute-start) | collective-permute-done | bytes 114720 | tf_op jit(solution)/shard_map/ppermute | solution.py:61
  50.7 4.1 %collective-permute-start.1 = (bf16[32,3584]{1,0:T(8,128)(2,1)S(1)}, bf16[32,3584]{1,0:T(8,128)(2,1)S(1)}, u32[]{:S(2)}, u32[]{:S(2)}) collective-permute-start(bf16[32,3584]{1,0:T(8,128)(2,1)S(1)} %pad_maximum_fusion), channel_id=1, source_target_pairs={{0,2},{1,3},{2,0},{3,1},{4,6},{5,7},{6,4},{7,5},{8,10},{9,11},{10,... | collective-permute-start | bytes 688136 | tf_op jit(solution)/shard_map/ppermute | solution.py:61
  54.8 0.1 reduce_window_sum.11
  54.8 0.1 copy.28
  54.9 0.1 copy.27
  55.0 0.1 eq.69
  55.1 0.1 fusion.36
  55.2 3.5 %collective-permute-done.1 = bf16[32,3584]{1,0:T(8,128)(2,1)S(1)} collective-permute-done((bf16[32,3584]{1,0:T(8,128)(2,1)S(1)}, bf16[32,3584]{1,0:T(8,128)(2,1)S(1)}, u32[]{:S(2)}, u32[]{:S(2)}) %collective-permute-start.1) | collective-permute-done | bytes 229408 | tf_op jit(solution)/shard_map/ppermute | solution.py:61
  58.8 2.1 convolution_convert_fusion
  61.0 86.4 %all_to_all.10 = bf16[8,4,16,7168]{3,2,1,0:T(8,128)(2,1)} all-to-all(bf16[8,4,16,7168]{3,2,1,0:T(8,128)(2,1)S(1)} %bitcast.54), channel_id=1, replica_groups=mesh['exp'=8,'tp'=4] {'exp'}, dimensions={0} | all-to-all | bytes 14680064 | tf_op jit(solution)/shard_map/all_to_all | solution.py:68
  147.4 13.5 %fusion.14 = f32[8,4,16,512]{3,2,0,1:T(8,128)S(1)} fusion(bf16[4,7168,512]{2,1,0:T(8,128)(2,1)} %param.15, bf16[8,4,16,7168]{3,2,1,0:T(8,128)(2,1)} %all_to_all.10), kind=kOutput, calls=%fused_computation.12 | convolution fusion | flops 3758096384 | bytes 37748736 | tf_op jit(solution)/shard_map/sicd,idh->sich/dot_general | solution.py:28
  160.9 15.5 %fusion.29 = bf16[8,4,16,512]{3,2,0,1:T(8,128)(2,1)S(1)} fusion(bf16[4,7168,512]{2,1,0:T(8,128)(2,1)} %param.16, bf16[8,4,16,7168]{3,2,1,0:T(8,128)(2,1)} %all_to_all.10, f32[8,4,16,512]{3,2,0,1:T(8,128)S(1)} %fusion.14), kind=kOutput, calls=%fused_computation.15 | convolution fusion | flops 3759669248 | bytes 38273024 | tf_op jit(solution)/shard_map/sicd,idh->sich/dot_general | solution.py:29
  176.4 16.3 %fusion.9 = bf16[8,4,16,7168]{3,2,0,1:T(8,128)(2,1)} fusion(bf16[8,4,16,512]{3,2,0,1:T(8,128)(2,1)S(1)} %fusion.29, bf16[4,512,7168]{2,1,0:T(8,128)(2,1)} %param.17), kind=kOutput, calls=%fused_computation.8 | convolution fusion | flops 3761766400 | bytes 37224448 | tf_op jit(solution)/shard_map/sich,ihd->sicd/dot_general | solution.py:31
  192.7 6.9 %copy.33 = bf16[8,4,16,7168]{3,2,1,0:T(8,128)(2,1)} copy(bf16[8,4,16,7168]{3,2,0,1:T(8,128)(2,1)} %fusion.9) | data formatting | bytes 14680064 | tf_op jit(solution)/shard_map/convert_element_type | solution.py:32
  199.6 4.8 %all-to-all-start.1 = ((bf16[8,4,16,7168]{3,2,1,0:T(8,128)(2,1)}), bf16[8,4,16,7168]{3,2,1,0:T(8,128)(2,1)}, u32[]{:S(2)}, u32[]{:S(2)}) async-start(bf16[8,4,16,7168]{3,2,1,0:T(8,128)(2,1)} %copy.33), calls=%async_computation.2 | async-start | bytes 14680064 | tf_op jit(solution)/shard_map/all_to_all | solution.py:73
  204.5 0.0 copy-start
  204.5 0.0 copy-start.1
  204.5 0.0 reduce-scatter.5.cloned.1.call-start
  204.6 0.1 copy.30
  204.6 0.1 select_convert_fusion
  204.7 82.6 %all-to-all-done.1 = bf16[8,4,16,7168]{3,2,1,0:T(8,128)(2,1)} async-done(((bf16[8,4,16,7168]{3,2,1,0:T(8,128)(2,1)}), bf16[8,4,16,7168]{3,2,1,0:T(8,128)(2,1)}, u32[]{:S(2)}, u32[]{:S(2)}) %all-to-all-start.1) | async-done | bytes 7340064 | tf_op jit(solution)/shard_map/all_to_all | solution.py:73
  287.3 5.3 %convolution_convert_fusion.1 = bf16[32,7168]{1,0:T(8,128)(2,1)} fusion(bf16[32,512]{0,1:T(8,128)(2,1)S(1)} %bitcast.55, bf16[512,7168]{1,0:T(8,128)(2,1)} %bitcast.15), kind=kOutput, calls=%fused_computation.9 | convolution fusion | flops 235110400 | bytes 7831552 | tf_op jit(solution)/shard_map/dot_general | solution.py:74
  292.5 0.0 reduce-scatter.5.cloned.1.call-update
  292.6 22.8 %reduce-scatter.5.cloned.1.call-done = bf16[32,1792]{1,0:T(8,128)(2,1)} async-done(((bf16[32,7168]{1,0:T(8,128)(2,1)}), bf16[32,1792]{1,0:T(8,128)(2,1)}) %reduce-scatter.5.cloned.1.call-update) | async-done | bytes 114704 | tf_op jit(solution)/shard_map/reduce_scatter | solution.py:77
  315.4 0.0 copy-done
  315.4 0.0 copy-done.1
  315.4 1.6 add_convert_fusion
  (12 shorter events, 0.1 us)
Async XLA Ops:
  6.5 26.8 %reduce-scatter.3.cloned.1.call-start = ((), (), s32[]{:S(2)}) async-start(), calls=%async_computation.4 | async-start | bytes 573440 | tf_op jit(solution)/shard_map/reduce_scatter | solution.py:43
  45.5 5.2 %collective-permute-start = (bf16[32,1792]{1,0:T(8,128)(2,1)S(1)}, bf16[32,1792]{1,0:T(8,128)(2,1)S(1)}, u32[]{:S(2)}, u32[]{:S(2)}) collective-permute-start(bf16[32,1792]{1,0:T(8,128)(2,1)S(1)} %get-tuple-element.10), channel_id=1, source_target_pairs={{0,3},{1,0},{2,1},{3,2},{4,7},{5,4},{6,5},{7,6},{8,11},{9,8},{10,9... | collective-permute-start | bytes 344072 | tf_op jit(solution)/shard_map/ppermute | solution.py:61
  50.7 8.1 %collective-permute-start.1 = (bf16[32,3584]{1,0:T(8,128)(2,1)S(1)}, bf16[32,3584]{1,0:T(8,128)(2,1)S(1)}, u32[]{:S(2)}, u32[]{:S(2)}) collective-permute-start(bf16[32,3584]{1,0:T(8,128)(2,1)S(1)} %pad_maximum_fusion), channel_id=1, source_target_pairs={{0,2},{1,3},{2,0},{3,1},{4,6},{5,7},{6,4},{7,5},{8,10},{9,11},{10,... | collective-permute-start | bytes 688136 | tf_op jit(solution)/shard_map/ppermute | solution.py:61
  199.6 87.7 %all-to-all-start.1 = ((bf16[8,4,16,7168]{3,2,1,0:T(8,128)(2,1)}), bf16[8,4,16,7168]{3,2,1,0:T(8,128)(2,1)}, u32[]{:S(2)}, u32[]{:S(2)}) async-start(bf16[8,4,16,7168]{3,2,1,0:T(8,128)(2,1)} %copy.33), calls=%async_computation.2 | async-start | bytes 14680064 | tf_op jit(solution)/shard_map/all_to_all | solution.py:73
  204.5 110.9 %copy-start = (bf16[32,1792]{1,0:T(8,128)(2,1)S(1)}, bf16[32,1792]{1,0:T(8,128)(2,1)}, u32[]{:S(2)}) copy-start(bf16[32,1792]{1,0:T(8,128)(2,1)} %param.10) | copy-start | bytes 344068
  204.5 110.9 %copy-start.1 = (bf16[32,1792]{1,0:T(8,128)(2,1)S(1)}, bf16[32,1792]{1,0:T(8,128)(2,1)}, u32[]{:S(2)}) copy-start(bf16[32,1792]{1,0:T(8,128)(2,1)} %reduce-scatter.3.cloned.1.call-done) | copy-start | bytes 344068
  204.5 110.9 %reduce-scatter.5.cloned.1.call-start = ((), (), s32[]{:S(2)}) async-start(), calls=%async_computation.5 | async-start | bytes 573440 | tf_op jit(solution)/shard_map/reduce_scatter | solution.py:77
Sparse Core Ops, SparseCore 0:
  9.6 23.6 reduce-scatter.2
  292.7 22.6 reduce-scatter.4
